TPU v7x, 128 devices: a whole 4x4x4 slice. The times are simulated.
128 devices in a mesh: store: 8 (over z_lo, y), mod: 16 (over z_hi, x, core).
Axes of the slice: x: 4, y: 4, z: 4 (z_hi: 2, z_lo: 2; z = z_hi * 2 + z_lo), core: 2. Of those that a mesh axis runs over, the one named last changes fastest.
Arguments:
- act_proj: bfloat16 [1024, 256, 1024], P(('store', 'mod')), may hold values from -1.5 to 1.5
- grad_proj: bfloat16 [1024, 256, 1024], P(('store', 'mod')), may hold values from -1.5 to 1.5
- token_mask: int32 [1024, 256], P(('store', 'mod')), may hold values 0 or 1
- layer_of: int32 [32], P('mod'), may hold values from 0 to 3, as said below
- layer_weight: float32 [4], replicated, may hold values from 0.25 to 4
- fisher_inv: bfloat16 [32, 1024, 1024], P('mod'), may hold values from -0.2 to 1.8
- stored_grads: bfloat16 [32768, 32768], P('store', 'mod'), may hold values from -0.049804688 to 0.049804688
Outputs:
- scores: float32 [1024, 32768], P('mod', 'store')
Inputs may be any that keep to these rules, and one draw needn't show every extreme that they name: `layer_of`: each of the 4 layers holds the same number of modules.
All inputs are finite; a program needn't handle non-finite values. No bound on the sum of `token_mask` on one device may be relied on, other than what follows from the above.
Results may differ from a plain program's by a relative error of at most 0.004.
Values may be sent and summed in bfloat16 or wider, within the bound.
No kernel may reach another device: no remote copies, remote signals or barrier semaphores. Data moves between devices by JAX's collectives and lax.ppermute only.
A program may use at most 128 MiB of HBM per device.

v0:
```python
import jax
import jax.numpy as jnp
from jax import lax
from jax.sharding import PartitionSpec as P

R = 32


def local(act_proj, grad_proj, token_mask, layer_of, layer_weight, fisher_inv, stored_grads):
    q_local, length, columns = act_proj.shape
    modules = columns // R
    valid_mask = token_mask.astype(jnp.bfloat16)[:, :, None]
    grad_side = (grad_proj * valid_mask).reshape(q_local, length, modules, R)
    act_side = act_proj.reshape(q_local, length, modules, R)
    per_sample = jnp.einsum(
        "qtmi,qtmj->qmij", grad_side, act_side, preferred_element_type=jnp.float32
    )
    per_sample = per_sample.reshape(q_local, modules, R * R).astype(jnp.bfloat16)
    picked = layer_of[:, None] == jnp.arange(layer_weight.shape[0], dtype=jnp.int32)[None, :]
    module_weight = jnp.sum(jnp.where(picked, layer_weight[None, :], 0.0), axis=1)
    grouped = lax.all_to_all(per_sample, "mod", split_axis=1, concat_axis=0, tiled=True)
    product = jnp.einsum("qkr,krc->qkc", grouped, fisher_inv, preferred_element_type=jnp.float32)
    conditioned = (product * module_weight[None, :, None]).astype(jnp.bfloat16)
    everyone = lax.all_gather(conditioned, "store", axis=0, tiled=True)
    flat_rows = everyone.reshape(everyone.shape[0], -1)
    return lax.psum_scatter(
        lax.dot_general(
            flat_rows, stored_grads, (((1,), (1,)), ((), ())), preferred_element_type=jnp.float32
        ),
        "mod",
        scatter_dimension=0,
        tiled=True,
    )


def solution(mesh):
    in_specs = (
        P(("store", "mod"), None, None),
        P(("store", "mod"), None, None),
        P(("store", "mod"), None),
        P("mod"),
        P(),
        P("mod", None, None),
        P("store", "mod"),
    )
    out_specs = P("mod", "store")
    return jax.shard_map(local, mesh=mesh, in_specs=in_specs, out_specs=out_specs, check_vma=False)
```

profile of v0, /device:TPU:0, one launch (start us, length us, event | category | flops | bytes accessed | tf_op | source)
XLA Modules:
  0.0 285.2 jit_solution(10545839637817417900)
XLA Ops:
  6.5 0.7 convert_element_type.15
  7.2 6.4 %copy.21 = bf16[8,256,1024]{1,2,0:T(8,128)(2,1)} copy(bf16[8,256,1024]{2,1,0:T(8,128)(2,1)} %param.7) | data formatting | bytes 8388608 | tf_op args[0]
  13.7 6.5 %copy.20 = bf16[8,256,1024]{1,2,0:T(8,128)(2,1)} copy(bf16[8,256,1024]{2,1,0:T(8,128)(2,1)} %param.8) | data formatting | bytes 8388608 | tf_op args[1]
  20.2 0.0 copy-start
  20.2 2.6 broadcast_multiply_fusion
  22.8 0.8 copy-done
  23.6 1.2 convolution_convert_fusion
  24.9 0.0 copy-start.1
  24.9 0.0 copy-start.2
  24.9 2.2 convert_element_type.17
  27.1 1.1 copy.22
  28.2 7.8 %all-to-all-start = ((bf16[8,32,1024]{2,0,1:T(8,128)(2,1)}), bf16[8,32,1024]{2,0,1:T(8,128)(2,1)S(1)}, u32[]{:S(2)}, u32[]{:S(2)}) async-start(bf16[8,32,1024]{2,0,1:T(8,128)(2,1)} %copy.22), calls=%async_computation | async-start | bytes 1048576 | tf_op jit(solution)/shard_map/all_to_all | solution.py:21
  36.0 0.0 all-gather.2.cloned.1.call-start
  36.1 0.0 copy-done.1
  36.1 0.0 copy-done.2
  36.1 0.2 fusion.4
  36.3 12.1 %all-to-all-done = bf16[8,32,1024]{2,0,1:T(8,128)(2,1)S(1)} async-done(((bf16[8,32,1024]{2,0,1:T(8,128)(2,1)}), bf16[8,32,1024]{2,0,1:T(8,128)(2,1)S(1)}, u32[]{:S(2)}, u32[]{:S(2)}) %all-to-all-start) | async-done | bytes 524320 | tf_op jit(solution)/shard_map/all_to_all | solution.py:21
  48.4 3.7 %fusion.1 = bf16[128,2,1024]{2,0,1:T(8,128)(2,1)} fusion(bf16[2,1024,1024]{2,1,0:T(8,128)(2,1)} %param.12, bf16[8,16,2,1024]{3,0,2,1:T(8,128)(2,1)S(1)} %bitcast.21, f32[2]{0:T(128)S(1)} %fusion.4), kind=kOutput, calls=%fused_computation.4 | convolution fusion | flops 537395200 | bytes 5242888 | tf_op jit(solution)/shard_map/qkr,krc->qkc/dot_general | solution.py:22
  52.1 0.0 all-gather.2.cloned.1.call-update
  52.1 0.0 reduce-scatter.2.cloned.1.call-start
  52.2 49.7 %all-gather.2.cloned.1.call-done = bf16[1024,2,1024]{2,0,1:T(8,128)(2,1)} async-done(((bf16[128,2,1024]{2,0,1:T(8,128)(2,1)}), bf16[1024,2,1024]{2,0,1:T(8,128)(2,1)}) %all-gather.2.cloned.1.call-update) | async-done | bytes 4194320 | tf_op jit(solution)/shard_map/all_gather | solution.py:24
  101.9 6.2 %copy.24 = bf16[1024,2,1024]{0,2,1:T(8,128)(2,1)} copy(bf16[1024,2,1024]{2,0,1:T(8,128)(2,1)} %all-gather.2.cloned.1.call-done) | data formatting | bytes 8388608 | tf_op jit(solution)/shard_map/all_gather | solution.py:24
  108.1 23.6 %fusion.5 = f32[1024,4096]{1,0:T(8,128)} fusion(bf16[1024,2048]{0,1:T(8,128)(2,1)} %bitcast.20, bf16[4096,2048]{1,0:T(8,128)(2,1)} %param.13), kind=kOutput, calls=%fused_computation.9 | convolution fusion | flops 17179869184 | bytes 37748736 | tf_op jit(solution)/shard_map/dot_general | solution.py:27
  131.7 0.0 reduce-scatter.2.cloned.1.call-update
  131.7 146.6 %reduce-scatter.2.cloned.1.call-done = f32[64,4096]{1,0:T(8,128)} async-done(((f32[1024,4096]{1,0:T(8,128)}), f32[64,4096]{1,0:T(8,128)}) %reduce-scatter.2.cloned.1.call-update) | async-done | bytes 1048592 | tf_op jit(solution)/shard_map/reduce_scatter | solution.py:26
Async XLA Ops:
  20.2 3.4 %copy-start = (bf16[8,256,1024]{1,2,0:T(8,128)(2,1)S(1)}, bf16[8,256,1024]{1,2,0:T(8,128)(2,1)}, u32[]{:S(2)}) copy-start(bf16[8,256,1024]{1,2,0:T(8,128)(2,1)} %copy.21) | copy-start | bytes 12582916
  24.9 11.2 %copy-start.1 = (f32[4]{0:T(128)S(1)}, f32[4]{0:T(128)}, u32[]{:S(2)}) copy-start(f32[4]{0:T(128)} %param.11) | copy-start | bytes 52
  24.9 11.2 %copy-start.2 = (s32[2]{0:T(128)S(1)}, s32[2]{0:T(128)}, u32[]{:S(2)}) copy-start(s32[2]{0:T(128)} %param.10) | copy-start | bytes 28
  28.2 20.2 %all-to-all-start = ((bf16[8,32,1024]{2,0,1:T(8,128)(2,1)}), bf16[8,32,1024]{2,0,1:T(8,128)(2,1)S(1)}, u32[]{:S(2)}, u32[]{:S(2)}) async-start(bf16[8,32,1024]{2,0,1:T(8,128)(2,1)} %copy.22), calls=%async_computation | async-start | bytes 1048576 | tf_op jit(solution)/shard_map/all_to_all | solution.py:21
  36.0 65.8 %all-gather.2.cloned.1.call-start = ((), (), s32[]{:S(2)}) async-start(), calls=%async_computation.2 | async-start | bytes 4718592 | tf_op jit(solution)/shard_map/all_gather | solution.py:24
  52.1 226.2 %reduce-scatter.2.cloned.1.call-start = ((), (), s32[]{:S(2)}) async-start(), calls=%async_computation.3 | async-start | bytes 17825792 | tf_op jit(solution)/shard_map/reduce_scatter | solution.py:26
Sparse Core Ops, SparseCore 0:
  52.2 49.5 all-gather.1
  131.8 146.4 reduce-scatter.1
where the time goes:
time: 286 us; the launch traced here: 285 us
  waiting for transfers between devices  208 us (73%)
  matrix products  28.5 us (10%)
  local copies, waits for them, and re-layouts  23.3 us (8%)
  between operations  13.5 us (5%)
  starting transfers between devices  7.91 us (3%)
  other arithmetic  3.49 us (1%)
    reduce_scatter x1, waiting for transfers between devices, local(): lax.psum_scatter(lax.dot_general(flat_rows, stored_grads, (((1,), (1,)),...  147 us
    all_gather x1, waiting for transfers between devices, local(): everyone = lax.all_gather(conditioned, 'store', axis=0, tiled=True)  49.7 us
    dot_general x1, matrix products, local(): lax.dot_general(flat_rows, stored_grads, (((1,), (1,)), ((), ())), prefer...  23.6 us
    unnamed x8, local copies, waits for them, and re-layouts  13.8 us
    all_to_all x1, waiting for transfers between devices, local(): lax.all_to_all(per_sample, 'mod', split_axis=1, concat_axis=0, tiled=True)  12.1 us
    all_to_all x1, starting transfers between devices, local(): lax.all_to_all(per_sample, 'mod', split_axis=1, concat_axis=0, tiled=True)  7.83 us
    all_gather x1, local copies, waits for them, and re-layouts, local(): everyone = lax.all_gather(conditioned, 'store', axis=0, tiled=True)  6.22 us
  transfers between devices with their start and end apart: 3, of which 3 were waited for; matrix products, arithmetic and copies ran while one was open for 0% of the time, Pallas kernels for 0%

commit v1 on v0

--- a/solution.py
+++ b/solution.py
@@ -18,7 +18,12 @@
     per_sample = per_sample.reshape(q_local, modules, R * R).astype(jnp.bfloat16)
     picked = layer_of[:, None] == jnp.arange(layer_weight.shape[0], dtype=jnp.int32)[None, :]
     module_weight = jnp.sum(jnp.where(picked, layer_weight[None, :], 0.0), axis=1)
-    grouped = lax.all_to_all(per_sample, "mod", split_axis=1, concat_axis=0, tiled=True)
+    grouped = jnp.concatenate(
+        lax.all_to_all(
+            jnp.stack(jnp.split(per_sample, lax.axis_size("mod"), axis=1), axis=0), "mod", 0, 0
+        ),
+        axis=0,
+    )
     product = jnp.einsum("qkr,krc->qkc", grouped, fisher_inv, preferred_element_type=jnp.float32)
     conditioned = (product * module_weight[None, :, None]).astype(jnp.bfloat16)
     everyone = lax.all_gather(conditioned, "store", axis=0, tiled=True)

time: 286 us -> 295 us (1.031)
  local copies, waits for them, and re-layouts: 23.3 us -> 32.6 us
    unnamed x8 -> x23, local copies, waits for them, and re-layouts: 13.8 us -> 23.5 us
where the time goes in v1:
time: 295 us; the launch traced here: 294 us
  waiting for transfers between devices  208 us (71%)
  local copies, waits for them, and re-layouts  32.6 us (11%)
  matrix products  28.6 us (10%)
  between operations  13.5 us (5%)
  starting transfers between devices  7.91 us (3%)
  other arithmetic  3.49 us (1%)
    reduce_scatter x1, waiting for transfers between devices, local(): lax.psum_scatter(lax.dot_general(flat_rows, stored_grads, (((1,), (1,)),...  147 us
    all_gather x1, waiting for transfers between devices, local(): everyone = lax.all_gather(conditioned, 'store', axis=0, tiled=True)  49.7 us
    dot_general x1, matrix products, local(): lax.dot_general(flat_rows, stored_grads, (((1,), (1,)), ((), ())), prefer...  23.6 us
    unnamed x23, local copies, waits for them, and re-layouts  23.5 us
    all_to_all x1, waiting for transfers between devices, local(): lax.all_to_all(jnp.stack(jnp.split(per_sample, lax.axis_size('mod'), axis...  12.1 us
    all_to_all x1, starting transfers between devices, local(): lax.all_to_all(jnp.stack(jnp.split(per_sample, lax.axis_size('mod'), axis...  7.83 us
    all_gather x1, local copies, waits for them, and re-layouts, local(): everyone = lax.all_gather(conditioned, 'store', axis=0, tiled=True)  6.22 us
  transfers between devices with their start and end apart: 3, of which 3 were waited for; matrix products, arithmetic and copies ran while one was open for 0% of the time, Pallas kernels for 0%

profile of v1, /device:TPU:0, one launch (start us, length us, event | category | flops | bytes accessed | tf_op | source)
XLA Modules:
  0.0 294.5 jit_solution(13858655958997649589)
XLA Ops:
  6.5 0.7 convert_element_type.15
  7.2 6.4 %copy.16 = bf16[8,256,1024]{1,2,0:T(8,128)(2,1)} copy(bf16[8,256,1024]{2,1,0:T(8,128)(2,1)} %param.7) | data formatting | bytes 8388608 | tf_op args[0]
  13.7 6.5 %copy.15 = bf16[8,256,1024]{1,2,0:T(8,128)(2,1)} copy(bf16[8,256,1024]{2,1,0:T(8,128)(2,1)} %param.8) | data formatting | bytes 8388608 | tf_op args[1]
  20.2 0.0 copy-start
  20.2 2.6 broadcast_multiply_fusion
  22.8 0.8 copy-done
  23.6 1.2 convolution_convert_fusion
  24.9 0.0 copy-start.1
  24.9 0.0 copy-start.2
  24.9 2.2 convert_element_type.17
  27.1 0.6 constant_dynamic-update-slice_fusion.15
  27.8 0.7 constant_dynamic-update-slice_fusion.14
  28.4 0.7 constant_dynamic-update-slice_fusion.13
  29.1 0.7 constant_dynamic-update-slice_fusion.12
  29.7 0.6 constant_dynamic-update-slice_fusion.11
  30.4 0.7 constant_dynamic-update-slice_fusion.10
  31.0 0.7 constant_dynamic-update-slice_fusion.9
  31.7 0.7 constant_dynamic-update-slice_fusion.8
  32.3 0.6 constant_dynamic-update-slice_fusion.7
  32.9 0.7 constant_dynamic-update-slice_fusion.6
  33.6 0.7 constant_dynamic-update-slice_fusion.5
  34.2 0.7 constant_dynamic-update-slice_fusion.4
  34.9 0.6 constant_dynamic-update-slice_fusion.3
  35.5 0.7 constant_dynamic-update-slice_fusion.2
  36.2 0.7 constant_dynamic-update-slice_fusion.1
  36.8 0.7 constant_dynamic-update-slice_fusion
  37.5 7.8 %all-to-all-start = ((bf16[16,8,2,1024]{3,2,1,0:T(2,128)(2,1)}), bf16[16,8,2,1024]{3,2,1,0:T(2,128)(2,1)S(1)}, u32[]{:S(2)}, u32[]{:S(2)}) async-start(bf16[16,8,2,1024]{3,2,1,0:T(2,128)(2,1)} %constant_dynamic-update-slice_fusion), calls=%async_computation | async-start | bytes 1048576 | tf_op jit(solution)/shard_map/all_to_all | solution.py:22
  45.3 0.0 all-gather.2.cloned.1.call-start
  45.4 0.0 copy-done.1
  45.4 0.0 copy-done.2
  45.4 0.2 fusion.4
  45.6 12.1 %all-to-all-done = bf16[16,8,2,1024]{3,2,1,0:T(2,128)(2,1)S(1)} async-done(((bf16[16,8,2,1024]{3,2,1,0:T(2,128)(2,1)}), bf16[16,8,2,1024]{3,2,1,0:T(2,128)(2,1)S(1)}, u32[]{:S(2)}, u32[]{:S(2)}) %all-to-all-start) | async-done | bytes 524320 | tf_op jit(solution)/shard_map/all_to_all | solution.py:22
  57.7 3.8 %fusion.1 = bf16[128,2,1024]{2,0,1:T(8,128)(2,1)} fusion(bf16[2,1024,1024]{2,1,0:T(8,128)(2,1)} %param.12, bf16[16,8,2,1024]{3,2,1,0:T(2,128)(2,1)S(1)} %all-to-all-done, f32[2]{0:T(128)S(1)} %fusion.4), kind=kOutput, calls=%fused_computation.4 | convolution fusion | flops 537395200 | bytes 5242888 | tf_op jit(solution)/shard_map/qkr,krc->qkc/dot_general | solution.py:27
  61.4 0.0 all-gather.2.cloned.1.call-update
  61.4 0.0 reduce-scatter.2.cloned.1.call-start
  61.5 49.7 %all-gather.2.cloned.1.call-done = bf16[1024,2,1024]{2,0,1:T(8,128)(2,1)} async-done(((bf16[128,2,1024]{2,0,1:T(8,128)(2,1)}), bf16[1024,2,1024]{2,0,1:T(8,128)(2,1)}) %all-gather.2.cloned.1.call-update) | async-done | bytes 4194320 | tf_op jit(solution)/shard_map/all_gather | solution.py:29
  111.2 6.2 %copy.18 = bf16[1024,2,1024]{0,2,1:T(8,128)(2,1)} copy(bf16[1024,2,1024]{2,0,1:T(8,128)(2,1)} %all-gather.2.cloned.1.call-done) | data formatting | bytes 8388608 | tf_op jit(solution)/shard_map/all_gather | solution.py:29
  117.4 23.6 %fusion.5 = f32[1024,4096]{1,0:T(8,128)} fusion(bf16[1024,2048]{0,1:T(8,128)(2,1)} %bitcast.81, bf16[4096,2048]{1,0:T(8,128)(2,1)} %param.13), kind=kOutput, calls=%fused_computation.41 | convolution fusion | flops 17179869184 | bytes 37748736 | tf_op jit(solution)/shard_map/dot_general | solution.py:32
  141.0 0.0 reduce-scatter.2.cloned.1.call-update
  141.0 146.6 %reduce-scatter.2.cloned.1.call-done = f32[64,4096]{1,0:T(8,128)} async-done(((f32[1024,4096]{1,0:T(8,128)}), f32[64,4096]{1,0:T(8,128)}) %reduce-scatter.2.cloned.1.call-update) | async-done | bytes 1048592 | tf_op jit(solution)/shard_map/reduce_scatter | solution.py:31
Async XLA Ops:
  20.2 3.4 %copy-start = (bf16[8,256,1024]{1,2,0:T(8,128)(2,1)S(1)}, bf16[8,256,1024]{1,2,0:T(8,128)(2,1)}, u32[]{:S(2)}) copy-start(bf16[8,256,1024]{1,2,0:T(8,128)(2,1)} %copy.16) | copy-start | bytes 12582916
  24.9 20.5 %copy-start.1 = (f32[4]{0:T(128)S(1)}, f32[4]{0:T(128)}, u32[]{:S(2)}) copy-start(f32[4]{0:T(128)} %param.11) | copy-start | bytes 52
  24.9 20.5 %copy-start.2 = (s32[2]{0:T(128)S(1)}, s32[2]{0:T(128)}, u32[]{:S(2)}) copy-start(s32[2]{0:T(128)} %param.10) | copy-start | bytes 28
  37.5 20.2 %all-to-all-start = ((bf16[16,8,2,1024]{3,2,1,0:T(2,128)(2,1)}), bf16[16,8,2,1024]{3,2,1,0:T(2,128)(2,1)S(1)}, u32[]{:S(2)}, u32[]{:S(2)}) async-start(bf16[16,8,2,1024]{3,2,1,0:T(2,128)(2,1)} %constant_dynamic-update-slice_fusion), calls=%async_computation | async-start | bytes 1048576 | tf_op jit(solution)/shard_map/all_to_all | solution.py:22
  45.3 65.9 %all-gather.2.cloned.1.call-start = ((), (), s32[]{:S(2)}) async-start(), calls=%async_computation.2 | async-start | bytes 4718592 | tf_op jit(solution)/shard_map/all_gather | solution.py:29
  61.4 226.2 %reduce-scatter.2.cloned.1.call-start = ((), (), s32[]{:S(2)}) async-start(), calls=%async_computation.3 | async-start | bytes 17825792 | tf_op jit(solution)/shard_map/reduce_scatter | solution.py:31
Sparse Core Ops, SparseCore 0:
  61.5 49.5 all-gather.1
  141.1 146.4 reduce-scatter.1
